TPU v7x, 512 devices: a whole 4x4x16 slice. The times are simulated.
512 devices in a mesh: fsdp: 128 (over y, z_lo, x), dp: 4 (over z_hi, core).
Axes of the slice: x: 4, y: 4, z: 16 (z_hi: 2, z_lo: 8; z = z_hi * 8 + z_lo), core: 2. Of those that a mesh axis runs over, the one named last changes fastest.
Arguments:
- tokens: bfloat16 [65536, 4096], P(('fsdp', 'dp')), may hold values from -6 to 6
- norm_gain: float32 [4096], replicated, may hold values from 0.25 to 1.75
- penalty: float32 [14336], P('dp'), may hold values from 0.25 to 4
- weight_tiles: bfloat16 [4, 384, 4096], P(None, 'fsdp'), may hold values from -0.375 to 0.375
- block_rows: int32 [224, 4], replicated, may hold values from 0 to 63, as said below
- block_slot: int32 [224, 4], replicated, may hold values from 0 to 383, as said below
Outputs:
- grad_tokens: bfloat16 [65536, 4096], P(('fsdp', 'dp'))
Inputs may be any that keep to these rules, and one draw needn't show every extreme that they name: `block_rows`: each block column names 4 distinct block rows. Within each run of 56 block columns (columns q * 56 to (q + 1) * 56 - 1), a block row is named at most 4 times, and some block row exactly 4 times. `block_slot`: within each run of 56 block columns, no slot is named twice. Slot s is stored by fsdp index s // 3; in each run some fsdp index has all 3 of its slots named.
All inputs are finite; a program needn't handle non-finite values.
Results may differ from a plain program's by a relative error of at most 0.014.
Values may be sent and summed in bfloat16 or wider, within the bound.
No kernel may reach another device: no remote copies, remote signals or barrier semaphores. Data moves between devices by JAX's collectives and lax.ppermute only.
A program may use at most 128 MiB of HBM per device.

v0:
```python
import jax
import jax.numpy as jnp
from jax import lax
from jax.experimental import pallas as pl
from jax.experimental.pallas import tpu as pltpu
from jax.sharding import Mesh
from jax.sharding import PartitionSpec as P

BLOCK = 64
HALF = BLOCK // 2
EPS = 1e-05
LANES = 128
GROUP = 28
ROWS = 32
NX, NY, NZ = 4, 4, 8
SIDE = 4
AXES = ("y", "zl", "x", "zh", "core")
SMEM = pl.BlockSpec(memory_space=pltpu.SMEM)
VMEM = pl.BlockSpec(memory_space=pltpu.VMEM)


def on_chip(x):
    return pltpu.with_memory_space_constraint(x, pltpu.VMEM)


def norm_kernel(tokens_ref, gain_ref, feat_ref, inverse_ref):
    x = tokens_ref[...].astype(jnp.float32)
    inverse = 1.0 / jnp.sqrt(jnp.mean(x * x, axis=1, keepdims=True) + EPS)
    inverse_ref[...] = inverse
    scaled = ((x * inverse) * gain_ref[...]).astype(jnp.bfloat16)
    for at in range(0, x.shape[1], LANES):
        feat_ref[at : at + LANES, :] = scaled[:, at : at + LANES].T


def invert_kernel(columns, per_column, tile_ref, row_ref, back_tile_ref, back_column_ref, count_ref):
    runs = 2
    blank = runs * SIDE * SIDE * NZ * 3
    spots = back_tile_ref.shape[0]

    def clear(i, carry):
        for j in range(4):
            back_tile_ref[4 * i + j] = blank
            back_column_ref[4 * i + j] = 0
        count_ref[i] = 0
        return carry

    lax.fori_loop(0, spots // 4, clear, 0)

    def note(column, carry):
        for k in range(per_column):
            at = column * per_column + k
            line = row_ref[at] + jnp.where(column < columns, 0, spots // 4 // runs)
            seen = count_ref[line]
            back_tile_ref[line * 4 + seen] = tile_ref[at]
            back_column_ref[line * 4 + seen] = column
            count_ref[line] = seen + 1
        return carry

    lax.fori_loop(0, runs * columns, note, 0)


def invert_call(columns, per_column, row_blocks, places, rows):
    spots = 2 * row_blocks * 4

    def body(*refs):
        invert_kernel(columns, per_column, *refs)

    return pl.pallas_call(
        body,
        out_shape=[jax.ShapeDtypeStruct((spots,), jnp.int32)] * 2,
        in_specs=[SMEM, SMEM],
        out_specs=[SMEM, SMEM],
        scratch_shapes=[pltpu.SMEM((spots // 4,), jnp.int32)],
        compiler_params=pltpu.CompilerParams(vmem_limit_bytes=1 << 20),
    )(places, rows)


def fill_kernel(pieces, *refs):
    parts, w_ref = refs[:-1], refs[-1]
    size = parts[0].shape[0]
    for piece, ref in zip(pieces, parts):
        w_ref[piece * size : (piece + 1) * size] = ref[...]
    w_ref[w_ref.shape[0] - 1] = jnp.zeros(w_ref.shape[1:], w_ref.dtype)


def fill_call(pieces, arrays):
    def body(*refs):
        fill_kernel(pieces, *refs)

    size, *tile = arrays[0].shape
    return pl.pallas_call(
        body,
        out_shape=pltpu.VMEM((2 * SIDE * size + 1, *tile), arrays[0].dtype),
        in_specs=[VMEM] * len(arrays),
        out_specs=VMEM,
        compiler_params=pltpu.CompilerParams(vmem_limit_bytes=1 << 20),
    )(*map(on_chip, arrays))


def back_row(tile_ref, column_ref, w_ref, grad_ref, row_blocks, row, lanes):
    left = lax.broadcasted_iota(jnp.int32, (HALF, 2 * BLOCK), 1) < BLOCK
    total = None
    for run in range(2):
        at = (run * row_blocks + row) * 4
        upper, lower = [], []
        for k in range(0, 4, 2):
            first, second = w_ref[tile_ref[at + k]], w_ref[tile_ref[at + k + 1]]
            upper.append(jnp.where(left, first, pltpu.roll(second, BLOCK, 1)))
            lower.append(jnp.where(left, pltpu.roll(first, BLOCK, 1), second))
        lhs = jnp.concatenate(
            [jnp.concatenate(upper, axis=1), jnp.concatenate(lower, axis=1)], axis=0
        )
        rhs = jnp.concatenate([grad_ref[column_ref[at + k], :, lanes] for k in range(4)], axis=0)
        part = jnp.dot(lhs, rhs, preferred_element_type=jnp.float32)
        total = part if total is None else total + part
    return total


def keep_kernel(tile_ref, column_ref, w_ref, grad_ref, keep_ref):
    row_blocks, _, count = keep_ref.shape

    def back(g, carry):
        for j in range(ROWS):
            row = g * ROWS + j
            keep_ref[row] = back_row(
                tile_ref, column_ref, w_ref, grad_ref, row_blocks, row, slice(0, count)
            )
        return carry

    lax.fori_loop(0, row_blocks // ROWS, back, 0)


def sparse_kernel(
    columns, per_column, tile_ref, row_ref, back_tile_ref, back_column_ref, unit_ref, mine_ref,
    other_ref, old_ref, first_ref, second_ref, w_ref, grad_ref, send_ref
):
    row_blocks, _, count = mine_ref.shape
    size = first_ref.shape[0]
    del old_ref
    for run, ref in enumerate((first_ref, second_ref)):
        at = (run * SIDE + 2) * size
        w_ref[at : at + size] = ref[...]

    def forward(g, j):
        at = (g * GROUP + j) * per_column
        rows = [row_ref[at + k] for k in range(per_column)]
        tiles = [w_ref[tile_ref[at + k]] for k in range(per_column)]
        turned = jnp.concatenate(tiles, axis=0).T
        lhs = jnp.concatenate([turned[:BLOCK], turned[BLOCK:]], axis=1)
        mine = [mine_ref[r] for r in rows]
        other = [other_ref[r] for r in rows]
        rhs = jnp.concatenate(
            [
                jnp.concatenate([p[:HALF] for p in side] + [p[HALF:] for p in side], axis=0)
                for side in (mine, other)
            ],
            axis=1,
        )
        preact = jnp.dot(lhs, rhs, preferred_element_type=jnp.float32)
        gating = jax.nn.sigmoid(preact)
        grad_act = unit_ref[g][:, j : j + 1] * (preact * gating)
        grad_pre = grad_act * (gating * (1.0 + preact * (1.0 - gating)))
        grad_ref[g * GROUP + j] = grad_pre.astype(jnp.bfloat16)

    def ahead(g, carry):
        for j in range(GROUP):
            forward(g, j)
        return carry

    def back(g, carry):
        for j in range(ROWS):
            row = g * ROWS + j
            send_ref[row] = back_row(
                back_tile_ref, back_column_ref, w_ref, grad_ref, row_blocks, row, slice(count, None)
            ).astype(jnp.bfloat16)
        return carry

    lax.fori_loop(0, 2 * columns // GROUP, ahead, 0)
    lax.fori_loop(0, row_blocks // ROWS, back, 0)


def close_kernel(keep_ref, came_ref, tokens_ref, gain_ref, inverse_ref, out_ref, grad_ref):
    inverse = inverse_ref[...]
    width = tokens_ref.shape[1]
    total = jnp.zeros((tokens_ref.shape[0], LANES), jnp.float32)
    for at in range(0, width, LANES):
        span = slice(at, at + LANES)
        grad = (keep_ref[span, :] + came_ref[span, :].astype(jnp.float32)).T
        grad = grad * gain_ref[:, span]
        grad_ref[:, span] = grad
        total += grad * (tokens_ref[:, span].astype(jnp.float32) * inverse)
    mixing = jnp.sum(total, axis=1, keepdims=True) * (1.0 / width)
    for at in range(0, width, LANES):
        span = slice(at, at + LANES)
        normed = tokens_ref[:, span].astype(jnp.float32) * inverse
        out_ref[:, span] = ((grad_ref[:, span] - normed * mixing) * inverse).astype(jnp.bfloat16)


def along_z(v, step):
    size = 2 * NZ
    pairs = []
    for z in range(size):
        for core in range(2):
            to = (z + (step if core == 0 else -step)) % size
            pairs.append([((at % NZ) * 2 + at // NZ) * 2 + core for at in (z, to)])
    return lax.ppermute(v, ("zl", "zh", "core"), pairs)


def along_side(v, step, leg):
    pairs = []
    for y in range(NY):
        for x in range(NX):
            for core in range(2):
                to_y, to_x = (y, (x + step) % NX) if core == leg else ((y + step) % NY, x)
                pairs.append(((y * NX + x) * 2 + core, (to_y * NX + to_x) * 2 + core))
    return lax.ppermute(v, ("y", "x", "core"), pairs)


def swap_cores(v):
    return lax.ppermute(v, "core", [(0, 1), (1, 0)])


def join_kernel(line_ref, ahead_ref, across_ref, back_ref, *plane_refs):
    size = line_ref.shape[1]
    for run, plane_ref in enumerate(plane_refs):
        for i, ref in enumerate((line_ref, ahead_ref, across_ref, back_ref)):
            plane_ref[i * size : (i + 1) * size] = ref[run]


def join(*parts):
    runs, size, *tile = parts[0].shape
    return pl.pallas_call(
        join_kernel,
        out_shape=[pltpu.VMEM((SIDE * size, *tile), parts[0].dtype)] * runs,
        in_specs=[VMEM] * len(parts),
        out_specs=[VMEM] * runs,
        compiler_params=pltpu.CompilerParams(vmem_limit_bytes=1 << 20),
    )(*map(on_chip, parts))


def of_core(table, core):
    paired = table.reshape(*table.shape[:-4], 2, 2, *table.shape[-3:])
    return lax.dynamic_index_in_dim(paired, core, paired.ndim - 4, keepdims=False)


def gather_tiles(own, core, early):
    _, slots = own.shape[:2]
    mine = of_core(own, core)
    far = along_z(own, 3)
    middle = along_z(own, 2)
    near = along_z(own, 1)
    opposite = along_z(of_core(middle, core), 2)
    near, middle, far, early = lax.optimization_barrier((near, middle, far, early))
    side = jnp.stack([near, middle, far])
    theirs = swap_cores(of_core(side, 1 - core))
    line = jnp.concatenate([mine[None], of_core(side, core), opposite[None], theirs], axis=0)
    line = line.transpose(1, 0, 2, 3, 4).reshape(2, NZ * slots, HALF, 2 * BLOCK)
    across, back, ahead = along_side(line, 2, 0), along_side(line, 1, 0), along_side(line, -1, 0)
    planes = join(line, ahead, across, back)
    back_0, ahead_1 = along_side(planes[0], 1, 1), along_side(planes[1], -1, 1)
    back_1, ahead_0 = along_side(planes[1], 1, 1), along_side(planes[0], -1, 1)
    across_0, across_1 = along_side(back_0, 1, 1), along_side(ahead_1, -1, 1)
    pieces = [planes[0], ahead_0, across_0, back_0, planes[1], ahead_1, across_1, back_1]
    return pieces, early


def tile_places(block_slot, slots, y, zl, x, core):
    owner, place = block_slot // slots, block_slot % slots
    step_x = (owner % NX - x) % NX
    step_z = ((owner // NX) % NZ - zl) * (2 * core - 1) % NZ
    step_z = jnp.where(step_z > NZ // 2, 3 * NZ // 2 - step_z, step_z)
    step_y = (owner // (NX * NZ) - y) % NY
    first = jnp.where(core == 0, step_x, step_y)
    second = jnp.where(core == 0, step_y, step_x)
    return ((second * SIDE + first) * NZ + step_z) * slots + place


def sparse_call(columns, per_column, places, rows, back_places, back_columns, units, mine, other, tiles):
    row_blocks, _, count = mine.shape
    late = (2, SIDE + 2)
    early = [i for i in range(len(tiles)) if i not in late]
    filled = fill_call(early, [tiles[i] for i in early])

    def body(*refs):
        sparse_kernel(columns, per_column, *refs)

    full, grads, send = pl.pallas_call(
        body,
        out_shape=(
            pltpu.VMEM(filled.shape, filled.dtype),
            pltpu.VMEM((2 * columns, BLOCK, 2 * count), jnp.bfloat16),
            pltpu.VMEM((row_blocks, BLOCK, count), jnp.bfloat16),
        ),
        in_specs=[SMEM] * 4 + [VMEM] * 6,
        out_specs=(VMEM, VMEM, VMEM),
        input_output_aliases={7: 0},
        compiler_params=pltpu.CompilerParams(vmem_limit_bytes=3 << 20),
    )(
        places, rows, back_places, back_columns, on_chip(units), on_chip(mine), on_chip(other),
        on_chip(filled), *(on_chip(tiles[i]) for i in late),
    )
    came = swap_cores(send)
    keep = pl.pallas_call(
        keep_kernel,
        out_shape=pltpu.VMEM((row_blocks, BLOCK, count), jnp.float32),
        in_specs=[SMEM] * 2 + [VMEM] * 2,
        out_specs=VMEM,
        compiler_params=pltpu.CompilerParams(vmem_limit_bytes=3 << 20),
    )(back_places, back_columns, on_chip(full), on_chip(grads))
    return keep, came


def norm_call(tokens, gain):
    count, width = tokens.shape
    return pl.pallas_call(
        norm_kernel,
        out_shape=(
            pltpu.VMEM((width, count), jnp.bfloat16),
            pltpu.VMEM((count, 1), jnp.float32),
        ),
        in_specs=[VMEM, VMEM],
        out_specs=(VMEM, VMEM),
        compiler_params=pltpu.CompilerParams(vmem_limit_bytes=6 << 20),
    )(on_chip(tokens), gain)


def close_call(keep, came, tokens, gain, inverse):
    count, width = tokens.shape
    return pl.pallas_call(
        close_kernel,
        out_shape=jax.ShapeDtypeStruct((count, width), jnp.bfloat16),
        in_specs=[VMEM] * 5,
        out_specs=VMEM,
        scratch_shapes=[pltpu.VMEM((count, width), jnp.float32)],
        compiler_params=pltpu.CompilerParams(vmem_limit_bytes=6 << 20),
    )(
        on_chip(keep.reshape(width, count)), on_chip(came.reshape(width, count)), on_chip(tokens),
        gain, on_chip(inverse),
    )


def unit_kernel(high_ref, near_ref, far_ref, units_ref):
    near, far, high = near_ref[...], far_ref[...], high_ref[0]
    groups = near.shape[0] // GROUP
    for run in range(2):
        turned = jnp.where(high == run, near, far).T
        for g in range(groups):
            units_ref[run * groups + g] = turned[:, g * GROUP : (g + 1) * GROUP]


def unit_call(high, near, far):
    columns, block = near.shape
    return pl.pallas_call(
        unit_kernel,
        out_shape=pltpu.VMEM((2 * columns // GROUP, block, GROUP), jnp.float32),
        in_specs=[SMEM, VMEM, VMEM],
        out_specs=VMEM,
        compiler_params=pltpu.CompilerParams(vmem_limit_bytes=1 << 20),
    )(high, on_chip(near), on_chip(far))


def pack_tiles(tiles):
    lead = tiles.shape[:-1]
    split = tiles.reshape(*lead, 2, HALF, BLOCK)
    return jnp.moveaxis(split, -3, -2).reshape(*lead, HALF, 2 * BLOCK)


def on_device(tokens, norm_gain, penalty, weight_tiles, block_rows, block_slot):
    y, zl, x, zh, core = (lax.axis_index(name) for name in AXES)
    runs, slots, _ = weight_tiles.shape
    count, width = tokens.shape
    columns, per_column = block_rows.shape[0] // runs, block_rows.shape[1]

    def of_runs(table):
        paired = table.reshape(2, 2, columns * per_column)
        return lax.dynamic_index_in_dim(paired, core, 1, keepdims=False).reshape(-1)

    rows = of_runs(block_rows)
    places = tile_places(block_slot, slots, y, zl, x, core).reshape(runs, columns * per_column)
    second = jnp.arange(runs)[:, None] // 2 * (NX * NY * NZ * slots)
    places = of_runs(places + second)
    near = penalty.reshape(columns, BLOCK)
    own = pack_tiles(weight_tiles)
    tiles, (rows, places, near, high) = gather_tiles(own, core, (rows, places, near, zh.reshape(1)))
    gain = norm_gain.reshape(1, width)
    features, inverse = norm_call(tokens, gain)
    other = swap_cores(features)
    distant = lax.ppermute(near, "zh", [(0, 1), (1, 0)])
    units = unit_call(high, near, distant)
    blocks = (width // BLOCK, BLOCK, count)
    back = invert_call(columns, per_column, width // BLOCK, places, rows)
    keep, came = sparse_call(
        columns, per_column, places, rows, *back, units, features.reshape(blocks), other.reshape(blocks), tiles
    )
    return close_call(keep, came, tokens, gain, inverse)


def solution(mesh):
    fine = Mesh(mesh.devices.reshape(NY, NZ, NX, 2, 2), AXES)
    placed = (P(AXES, None), P(), P(("zh", "core")), P(None, ("y", "zl", "x"), None), P(), P())

    return jax.shard_map(on_device, mesh=fine, in_specs=placed, out_specs=P(AXES, None), check_vma=False)
```

profile of v0, /device:TPU:1, one launch (start us, length us, event | category | flops | bytes accessed | tf_op | source)
XLA Modules:
  0.0 114.4 jit_solution(2770291512663944042)
XLA Ops:
  0.0 0.0 copy-start
  0.0 0.0 copy-start.1
  0.0 1.2 %reshape.104 = bf16[4,3,2,32,64]{4,3,2,0,1:T(8,128)(2,1)S(1)} reshape(bf16[4,3,4096]{2,0,1:T(4,128)(2,1)} %param.9) | data formatting | bytes 196608 | tf_op jit(solution)/shard_map/reshape | solution.py:364
  1.2 0.2 copy.16
  1.4 0.1 reshape.105
  1.5 12.8 %collective-permute-start.2 = (bf16[4,3,32,128]{3,2,1,0:T(8,128)(2,1)S(1)}, bf16[4,3,32,128]{3,2,1,0:T(8,128)(2,1)S(1)}, u32[]{:S(2)}, u32[]{:S(2)}) collective-permute-start(bf16[4,3,32,128]{3,2,1,0:T(8,128)(2,1)S(1)} %reshape.105), channel_id=1, source_target_pairs={{0,48},{1,83},{16,64},{17,99},{32,80},{33,115},{48,96},{49,1},{64,... | collective-permute-start | bytes 294920 | tf_op jit(solution)/shard_map/ppermute | solution.py:206
  14.4 4.3 %collective-permute-start.1 = (bf16[4,3,32,128]{3,2,1,0:T(8,128)(2,1)S(1)}, bf16[4,3,32,128]{3,2,1,0:T(8,128)(2,1)S(1)}, u32[]{:S(2)}, u32[]{:S(2)}) collective-permute-start(bf16[4,3,32,128]{3,2,1,0:T(8,128)(2,1)S(1)} %reshape.105), channel_id=1, source_target_pairs={{0,32},{1,99},{16,48},{17,115},{32,64},{33,1},{48,80},{49,17},{64,... | collective-permute-start | bytes 294920 | tf_op jit(solution)/shard_map/ppermute | solution.py:206
  18.7 2.6 %collective-permute-start = (bf16[4,3,32,128]{3,2,1,0:T(8,128)(2,1)S(1)}, bf16[4,3,32,128]{3,2,1,0:T(8,128)(2,1)S(1)}, u32[]{:S(2)}, u32[]{:S(2)}) collective-permute-start(bf16[4,3,32,128]{3,2,1,0:T(8,128)(2,1)S(1)} %reshape.105), channel_id=1, source_target_pairs={{0,16},{1,115},{16,32},{17,1},{32,48},{33,17},{48,64},{49,33},{64,... | collective-permute-start | bytes 294920 | tf_op jit(solution)/shard_map/ppermute | solution.py:206
  21.3 0.1 reshape_reshape.3
  21.5 0.8 reshape.110.near_ref
  22.3 0.7 fusion.9
  23.0 0.1 copy.13
  23.1 0.1 reshape.108
  23.2 0.8 copy.12
  24.1 0.1 reshape.106
  24.2 0.1 constant_dynamic-slice_fusion
  24.3 0.1 fusion.14
  24.3 0.1 reshape.109.refs_0_
  24.4 0.1 reshape.107.refs_1_
  24.5 0.0 collective-permute-done.2
  24.5 0.0 collective-permute-done.1
  24.5 0.0 collective-permute-done
  24.6 1.9 %collective-permute-start.6 = (bf16[3,2,3,32,128]{4,3,2,1,0:T(8,128)(2,1)S(1)}, bf16[3,2,3,32,128]{4,3,2,1,0:T(8,128)(2,1)S(1)}, u32[]{:S(2)}, u32[]{:S(2)}) collective-permute-start(bf16[3,2,3,32,128]{4,3,2,1,0:T(8,128)(2,1)S(1)} %get-tuple-element.38), channel_id=1, source_target_pairs={{0,1},{1,0},{2,3},{3,2},{4,5},{5,4},{6,7},{7,6},{8,9},{9,8},{10,11... | collective-permute-start | bytes 442376 | tf_op jit(solution)/shard_map/ppermute | solution.py:220
  26.6 3.1 %collective-permute-start.5 = (bf16[2,3,32,128]{3,2,1,0:T(8,128)(2,1)S(1)}, bf16[2,3,32,128]{3,2,1,0:T(8,128)(2,1)S(1)}, u32[]{:S(2)}, u32[]{:S(2)}) collective-permute-start(bf16[2,3,32,128]{3,2,1,0:T(8,128)(2,1)S(1)} %dynamic-slice_bitcast_fusion.2), channel_id=1, source_target_pairs={{0,32},{1,99},{16,48},{17,115},{32,64},{33,1},{48,80},{49,17},{64,... | collective-permute-start | bytes 147464 | tf_op jit(solution)/shard_map/ppermute | solution.py:206
  29.7 3.0 %collective-permute-done.5 = bf16[2,3,32,128]{3,2,1,0:T(8,128)(2,1)S(1)} collective-permute-done((bf16[2,3,32,128]{3,2,1,0:T(8,128)(2,1)S(1)}, bf16[2,3,32,128]{3,2,1,0:T(8,128)(2,1)S(1)}, u32[]{:S(2)}, u32[]{:S(2)}) %collective-permute-start.5) | collective-permute-done | bytes 49184 | tf_op jit(solution)/shard_map/ppermute | solution.py:206
  32.7 0.0 collective-permute-done.6
  32.7 0.1 maximum_bitcast_fusion
  32.8 3.2 %collective-permute-start.9 = (bf16[2,24,32,128]{3,2,1,0:T(8,128)(2,1)S(1)}, bf16[2,24,32,128]{3,2,1,0:T(8,128)(2,1)S(1)}, u32[]{:S(2)}, u32[]{:S(2)}) collective-permute-start(bf16[2,24,32,128]{3,2,1,0:T(8,128)(2,1)S(1)} %bitcast.28), channel_id=1, source_target_pairs={{0,4},{1,129},{4,8},{5,133},{8,12},{9,137},{12,0},{13,141},{128,13... | collective-permute-start | bytes 1179656 | tf_op jit(solution)/shard_map/ppermute | solution.py:216
  36.0 4.5 %collective-permute-start.8 = (bf16[2,24,32,128]{3,2,1,0:T(8,128)(2,1)S(1)}, bf16[2,24,32,128]{3,2,1,0:T(8,128)(2,1)S(1)}, u32[]{:S(2)}, u32[]{:S(2)}) collective-permute-start(bf16[2,24,32,128]{3,2,1,0:T(8,128)(2,1)S(1)} %bitcast.29), channel_id=1, source_target_pairs={{0,8},{1,257},{4,12},{5,261},{8,0},{9,265},{12,4},{13,269},{128,13... | collective-permute-start | bytes 1179656 | tf_op jit(solution)/shard_map/ppermute | solution.py:216
  40.6 3.0 %collective-permute-start.7 = (bf16[2,24,32,128]{3,2,1,0:T(8,128)(2,1)S(1)}, bf16[2,24,32,128]{3,2,1,0:T(8,128)(2,1)S(1)}, u32[]{:S(2)}, u32[]{:S(2)}) collective-permute-start(bf16[2,24,32,128]{3,2,1,0:T(8,128)(2,1)S(1)} %bitcast.30), channel_id=1, source_target_pairs={{0,12},{1,385},{4,0},{5,389},{8,4},{9,393},{12,8},{13,397},{128,14... | collective-permute-start | bytes 1179656 | tf_op jit(solution)/shard_map/ppermute | solution.py:216
  43.5 0.0 collective-permute-done.9.back_ref
  43.6 4.7 %collective-permute-done.8.across_ref = bf16[2,24,32,128]{3,2,1,0:T(8,128)(2,1)S(1)} collective-permute-done((bf16[2,24,32,128]{3,2,1,0:T(8,128)(2,1)S(1)}, bf16[2,24,32,128]{3,2,1,0:T(8,128)(2,1)S(1)}, u32[]{:S(2)}, u32[]{:S(2)}) %collective-permute-start.8) | collective-permute-done | bytes 393248 | tf_op jit(solution)/shard_map/ppermute | solution.py:216
  48.3 1.3 %collective-permute-done.7.ahead_ref = bf16[2,24,32,128]{3,2,1,0:T(8,128)(2,1)S(1)} collective-permute-done((bf16[2,24,32,128]{3,2,1,0:T(8,128)(2,1)S(1)}, bf16[2,24,32,128]{3,2,1,0:T(8,128)(2,1)S(1)}, u32[]{:S(2)}, u32[]{:S(2)}) %collective-permute-start.7) | collective-permute-done | bytes 393248 | tf_op jit(solution)/shard_map/ppermute | solution.py:216
  49.6 0.1 shard_map.67
  49.7 3.1 %collective-permute-start.11 = (bf16[96,32,128]{2,1,0:T(8,128)(2,1)S(1)}, bf16[96,32,128]{2,1,0:T(8,128)(2,1)S(1)}, u32[]{:S(2)}, u32[]{:S(2)}) collective-permute-start(bf16[96,32,128]{2,1,0:T(8,128)(2,1)S(1)} %get-tuple-element.31.refs_0_), channel_id=1, source_target_pairs={{0,128},{1,5},{4,132},{5,9},{8,136},{9,13},{12,140},{13,1},{128,25... | collective-permute-start | bytes 2359304 | tf_op jit(solution)/shard_map/ppermute | solution.py:216
  52.9 3.4 %collective-permute-start.12 = (bf16[96,32,128]{2,1,0:T(8,128)(2,1)S(1)}, bf16[96,32,128]{2,1,0:T(8,128)(2,1)S(1)}, u32[]{:S(2)}, u32[]{:S(2)}) collective-permute-start(bf16[96,32,128]{2,1,0:T(8,128)(2,1)S(1)} %get-tuple-element.32.refs_3_), channel_id=1, source_target_pairs={{0,384},{1,13},{4,388},{5,1},{8,392},{9,5},{12,396},{13,9},{128,0}... | collective-permute-start | bytes 2359304 | tf_op jit(solution)/shard_map/ppermute | solution.py:216
  56.2 0.0 copy-done
  56.2 0.0 copy-done.1
  56.3 0.6 shard_map.66
  56.9 6.5 %collective-permute-start.4 = (bf16[4096,128]{1,0:T(8,128)(2,1)S(1)}, bf16[4096,128]{1,0:T(8,128)(2,1)S(1)}, u32[]{:S(2)}, u32[]{:S(2)}) collective-permute-start(bf16[4096,128]{1,0:T(8,128)(2,1)S(1)} %get-tuple-element.27), channel_id=1, source_target_pairs={{0,1},{1,0},{2,3},{3,2},{4,5},{5,4},{6,7},{7,6},{8,9},{9,8},{10,11... | collective-permute-start | bytes 3145736 | tf_op jit(solution)/shard_map/ppermute | solution.py:220
  63.4 7.9 %collective-permute-start.3 = (f32[56,64]{1,0:T(8,128)S(1)}, f32[56,64]{1,0:T(8,128)S(1)}, u32[]{:S(2)}, u32[]{:S(2)}) collective-permute-start(f32[56,64]{1,0:T(8,128)S(1)} %reshape.110.near_ref), channel_id=1, source_target_pairs={{0,2},{2,0},{1,3},{3,1},{4,6},{6,4},{5,7},{7,5},{8,10},{10,8},{9,1... | collective-permute-start | bytes 43016 | tf_op jit(solution)/shard_map/ppermute | solution.py:388
  71.2 4.3 %collective-permute-start.10 = (bf16[96,32,128]{2,1,0:T(8,128)(2,1)S(1)}, bf16[96,32,128]{2,1,0:T(8,128)(2,1)S(1)}, u32[]{:S(2)}, u32[]{:S(2)}) collective-permute-start(bf16[96,32,128]{2,1,0:T(8,128)(2,1)S(1)} %get-tuple-element.31.refs_0_), channel_id=1, source_target_pairs={{0,384},{1,13},{4,388},{5,1},{8,392},{9,5},{12,396},{13,9},{128,0}... | collective-permute-start | bytes 2359304 | tf_op jit(solution)/shard_map/ppermute | solution.py:216
  75.5 1.2 %collective-permute-done.3.far_ref = f32[56,64]{1,0:T(8,128)S(1)} collective-permute-done((f32[56,64]{1,0:T(8,128)S(1)}, f32[56,64]{1,0:T(8,128)S(1)}, u32[]{:S(2)}, u32[]{:S(2)}) %collective-permute-start.3) | collective-permute-done | bytes 14368 | tf_op jit(solution)/shard_map/ppermute | solution.py:388
  76.7 4.0 %collective-permute-start.13 = (bf16[96,32,128]{2,1,0:T(8,128)(2,1)S(1)}, bf16[96,32,128]{2,1,0:T(8,128)(2,1)S(1)}, u32[]{:S(2)}, u32[]{:S(2)}) collective-permute-start(bf16[96,32,128]{2,1,0:T(8,128)(2,1)S(1)} %get-tuple-element.32.refs_3_), channel_id=1, source_target_pairs={{0,128},{1,5},{4,132},{5,9},{8,136},{9,13},{12,140},{13,1},{128,25... | collective-permute-start | bytes 2359304 | tf_op jit(solution)/shard_map/ppermute | solution.py:216
  80.8 0.0 collective-permute-done.11.refs_2_
  80.8 2.2 %collective-permute-start.14 = (bf16[96,32,128]{2,1,0:T(8,128)(2,1)S(1)}, bf16[96,32,128]{2,1,0:T(8,128)(2,1)S(1)}, u32[]{:S(2)}, u32[]{:S(2)}) collective-permute-start(bf16[96,32,128]{2,1,0:T(8,128)(2,1)S(1)} %collective-permute-done.11.refs_2_), channel_id=1, source_target_pairs={{0,128},{1,5},{4,132},{5,9},{8,136},{9,13},{12,140},{13,1},{128,25... | collective-permute-start | bytes 2359304 | tf_op jit(solution)/shard_map/ppermute | solution.py:216
  83.0 0.0 collective-permute-done.12.refs_4_
  83.0 4.3 %collective-permute-start.15 = (bf16[96,32,128]{2,1,0:T(8,128)(2,1)S(1)}, bf16[96,32,128]{2,1,0:T(8,128)(2,1)S(1)}, u32[]{:S(2)}, u32[]{:S(2)}) collective-permute-start(bf16[96,32,128]{2,1,0:T(8,128)(2,1)S(1)} %collective-permute-done.12.refs_4_), channel_id=1, source_target_pairs={{0,384},{1,13},{4,388},{5,1},{8,392},{9,5},{12,396},{13,9},{128,0}... | collective-permute-start | bytes 2359304 | tf_op jit(solution)/shard_map/ppermute | solution.py:216
  87.3 6.2 %shard_map.64 = (s32[512]{0:T(512)S(1)}, s32[512]{0:T(512)S(1)}) custom-call(s32[448]{0:T(512)S(1)} %reshape.109.refs_0_, s32[448]{0:T(512)S(1)} %reshape.107.refs_1_), custom_call_target="tpu_custom_call" | custom-call | tf_op jit(solution)/shard_map/pallas_call | solution.py:68
  93.5 0.2 shard_map.65.refs_4_
  93.7 0.0 collective-permute-done.10.refs_1_
  93.7 0.0 collective-permute-done.13.refs_5_
  93.7 0.3 shard_map.68.refs_7_
  94.0 0.0 collective-permute-done.4
  94.0 5.4 %collective-permute-done.14.refs_8_ = bf16[96,32,128]{2,1,0:T(8,128)(2,1)S(1)} collective-permute-done((bf16[96,32,128]{2,1,0:T(8,128)(2,1)S(1)}, bf16[96,32,128]{2,1,0:T(8,128)(2,1)S(1)}, u32[]{:S(2)}, u32[]{:S(2)}) %collective-permute-start.14) | collective-permute-done | bytes 786464 | tf_op jit(solution)/shard_map/ppermute | solution.py:216
  99.4 0.0 collective-permute-done.15.refs_9_
  99.4 6.2 %shard_map.69 = (bf16[769,32,128]{2,1,0:T(8,128)(2,1)S(1)}, bf16[112,64,256]{2,1,0:T(8,128)(2,1)S(1)}, bf16[64,64,128]{2,1,0:T(8,128)(2,1)S(1)}) custom-call(s32[448]{0:T(512)S(1)} %reshape.109.refs_0_, s32[448]{0:T(512)S(1)} %reshape.107.refs_1_, s32[512]{0:T(512)S(1)} %get-tuple-element.23.refs_2_.tile_ref, ...), custom_call_target="tpu_custom_call", output_to_operand_aliasing={{0}: (7, {})} | custom-call | tf_op jit(solution)/shard_map/pallas_call | solution.py:287
  105.6 3.9 %collective-permute-start.16 = (bf16[64,64,128]{2,1,0:T(8,128)(2,1)S(1)}, bf16[64,64,128]{2,1,0:T(8,128)(2,1)S(1)}, u32[]{:S(2)}, u32[]{:S(2)}) collective-permute-start(bf16[64,64,128]{2,1,0:T(8,128)(2,1)S(1)} %get-tuple-element.35), channel_id=1, source_target_pairs={{0,1},{1,0},{2,3},{3,2},{4,5},{5,4},{6,7},{7,6},{8,9},{9,8},{10,11... | collective-permute-start | bytes 3145736 | tf_op jit(solution)/shard_map/ppermute | solution.py:220
  109.5 2.6 %shard_map.70 = f32[64,64,128]{2,1,0:T(8,128)S(1)} custom-call(s32[512]{0:T(512)S(1)} %get-tuple-element.23.refs_2_.tile_ref, s32[512]{0:T(512)S(1)} %get-tuple-element.24.refs_3_.column_ref, bf16[769,32,128]{2,1,0:T(8,128)(2,1)S(1)} %get-tuple-element.33.w_ref, bf16[112,64,256]{2,1,0:T(8,128)(2,1)S(1)} %get-tuple-element.34.grad_ref), custom_call_target="tpu_custom_call" | custom-call | tf_op jit(solution)/shard_map/pallas_call | solution.py:303
  112.2 0.0 collective-permute-done.16
  112.2 2.2 %shard_map.71 = bf16[128,4096]{1,0:T(8,128)(2,1)} custom-call(f32[4096,128]{1,0:T(8,128)S(1)} %bitcast.27, bf16[4096,128]{1,0:T(8,128)(2,1)S(1)} %bitcast.34, bf16[128,4096]{1,0:T(8,128)(2,1)S(1)} %copy-done, f32[1,4096]{1,0:T(1,128)S(1)} %bitcast.36, f32[128,1]{1,0:T(8,128)S(1)} %get-tuple-element.36.inverse_ref), custom_call_target="tpu_custom_call" | custom-call | tf_op jit(solution)/shard_map/pallas_call | solution.py:329
  (6 shorter events, 0.1 us)
Async XLA Ops:
  0.0 56.2 %copy-start = (bf16[128,4096]{1,0:T(8,128)(2,1)S(1)}, bf16[128,4096]{1,0:T(8,128)(2,1)}, u32[]{:S(2)}) copy-start(bf16[128,4096]{1,0:T(8,128)(2,1)} %tokens_ref.3) | copy-start | bytes 3145732
  0.0 56.2 %copy-start.1 = (f32[4096]{0:T(1024)S(1)}, f32[4096]{0:T(1024)}, u32[]{:S(2)}) copy-start(f32[4096]{0:T(1024)} %param.7) | copy-start | bytes 49156
  1.5 23.0 %collective-permute-start.2 = (bf16[4,3,32,128]{3,2,1,0:T(8,128)(2,1)S(1)}, bf16[4,3,32,128]{3,2,1,0:T(8,128)(2,1)S(1)}, u32[]{:S(2)}, u32[]{:S(2)}) collective-permute-start(bf16[4,3,32,128]{3,2,1,0:T(8,128)(2,1)S(1)} %reshape.105), channel_id=1, source_target_pairs={{0,48},{1,83},{16,64},{17,99},{32,80},{33,115},{48,96},{49,1},{64,... | collective-permute-start | bytes 294920 | tf_op jit(solution)/shard_map/ppermute | solution.py:206
  14.4 10.2 %collective-permute-start.1 = (bf16[4,3,32,128]{3,2,1,0:T(8,128)(2,1)S(1)}, bf16[4,3,32,128]{3,2,1,0:T(8,128)(2,1)S(1)}, u32[]{:S(2)}, u32[]{:S(2)}) collective-permute-start(bf16[4,3,32,128]{3,2,1,0:T(8,128)(2,1)S(1)} %reshape.105), channel_id=1, source_target_pairs={{0,32},{1,99},{16,48},{17,115},{32,64},{33,1},{48,80},{49,17},{64,... | collective-permute-start | bytes 294920 | tf_op jit(solution)/shard_map/ppermute | solution.py:206
  18.7 5.9 %collective-permute-start = (bf16[4,3,32,128]{3,2,1,0:T(8,128)(2,1)S(1)}, bf16[4,3,32,128]{3,2,1,0:T(8,128)(2,1)S(1)}, u32[]{:S(2)}, u32[]{:S(2)}) collective-permute-start(bf16[4,3,32,128]{3,2,1,0:T(8,128)(2,1)S(1)} %reshape.105), channel_id=1, source_target_pairs={{0,16},{1,115},{16,32},{17,1},{32,48},{33,17},{48,64},{49,33},{64,... | collective-permute-start | bytes 294920 | tf_op jit(solution)/shard_map/ppermute | solution.py:206
  24.6 8.1 %collective-permute-start.6 = (bf16[3,2,3,32,128]{4,3,2,1,0:T(8,128)(2,1)S(1)}, bf16[3,2,3,32,128]{4,3,2,1,0:T(8,128)(2,1)S(1)}, u32[]{:S(2)}, u32[]{:S(2)}) collective-permute-start(bf16[3,2,3,32,128]{4,3,2,1,0:T(8,128)(2,1)S(1)} %get-tuple-element.38), channel_id=1, source_target_pairs={{0,1},{1,0},{2,3},{3,2},{4,5},{5,4},{6,7},{7,6},{8,9},{9,8},{10,11... | collective-permute-start | bytes 442376 | tf_op jit(solution)/shard_map/ppermute | solution.py:220
  26.6 6.2 %collective-permute-start.5 = (bf16[2,3,32,128]{3,2,1,0:T(8,128)(2,1)S(1)}, bf16[2,3,32,128]{3,2,1,0:T(8,128)(2,1)S(1)}, u32[]{:S(2)}, u32[]{:S(2)}) collective-permute-start(bf16[2,3,32,128]{3,2,1,0:T(8,128)(2,1)S(1)} %dynamic-slice_bitcast_fusion.2), channel_id=1, source_target_pairs={{0,32},{1,99},{16,48},{17,115},{32,64},{33,1},{48,80},{49,17},{64,... | collective-permute-start | bytes 147464 | tf_op jit(solution)/shard_map/ppermute | solution.py:206
  32.8 10.7 %collective-permute-start.9 = (bf16[2,24,32,128]{3,2,1,0:T(8,128)(2,1)S(1)}, bf16[2,24,32,128]{3,2,1,0:T(8,128)(2,1)S(1)}, u32[]{:S(2)}, u32[]{:S(2)}) collective-permute-start(bf16[2,24,32,128]{3,2,1,0:T(8,128)(2,1)S(1)} %bitcast.28), channel_id=1, source_target_pairs={{0,4},{1,129},{4,8},{5,133},{8,12},{9,137},{12,0},{13,141},{128,13... | collective-permute-start | bytes 1179656 | tf_op jit(solution)/shard_map/ppermute | solution.py:216
  36.0 12.3 %collective-permute-start.8 = (bf16[2,24,32,128]{3,2,1,0:T(8,128)(2,1)S(1)}, bf16[2,24,32,128]{3,2,1,0:T(8,128)(2,1)S(1)}, u32[]{:S(2)}, u32[]{:S(2)}) collective-permute-start(bf16[2,24,32,128]{3,2,1,0:T(8,128)(2,1)S(1)} %bitcast.29), channel_id=1, source_target_pairs={{0,8},{1,257},{4,12},{5,261},{8,0},{9,265},{12,4},{13,269},{128,13... | collective-permute-start | bytes 1179656 | tf_op jit(solution)/shard_map/ppermute | solution.py:216
  40.6 9.1 %collective-permute-start.7 = (bf16[2,24,32,128]{3,2,1,0:T(8,128)(2,1)S(1)}, bf16[2,24,32,128]{3,2,1,0:T(8,128)(2,1)S(1)}, u32[]{:S(2)}, u32[]{:S(2)}) collective-permute-start(bf16[2,24,32,128]{3,2,1,0:T(8,128)(2,1)S(1)} %bitcast.30), channel_id=1, source_target_pairs={{0,12},{1,385},{4,0},{5,389},{8,4},{9,393},{12,8},{13,397},{128,14... | collective-permute-start | bytes 1179656 | tf_op jit(solution)/shard_map/ppermute | solution.py:216
  49.7 31.1 %collective-permute-start.11 = (bf16[96,32,128]{2,1,0:T(8,128)(2,1)S(1)}, bf16[96,32,128]{2,1,0:T(8,128)(2,1)S(1)}, u32[]{:S(2)}, u32[]{:S(2)}) collective-permute-start(bf16[96,32,128]{2,1,0:T(8,128)(2,1)S(1)} %get-tuple-element.31.refs_0_), channel_id=1, source_target_pairs={{0,128},{1,5},{4,132},{5,9},{8,136},{9,13},{12,140},{13,1},{128,25... | collective-permute-start | bytes 2359304 | tf_op jit(solution)/shard_map/ppermute | solution.py:216
  52.9 30.2 %collective-permute-start.12 = (bf16[96,32,128]{2,1,0:T(8,128)(2,1)S(1)}, bf16[96,32,128]{2,1,0:T(8,128)(2,1)S(1)}, u32[]{:S(2)}, u32[]{:S(2)}) collective-permute-start(bf16[96,32,128]{2,1,0:T(8,128)(2,1)S(1)} %get-tuple-element.32.refs_3_), channel_id=1, source_target_pairs={{0,384},{1,13},{4,388},{5,1},{8,392},{9,5},{12,396},{13,9},{128,0}... | collective-permute-start | bytes 2359304 | tf_op jit(solution)/shard_map/ppermute | solution.py:216
  56.9 37.1 %collective-permute-start.4 = (bf16[4096,128]{1,0:T(8,128)(2,1)S(1)}, bf16[4096,128]{1,0:T(8,128)(2,1)S(1)}, u32[]{:S(2)}, u32[]{:S(2)}) collective-permute-start(bf16[4096,128]{1,0:T(8,128)(2,1)S(1)} %get-tuple-element.27), channel_id=1, source_target_pairs={{0,1},{1,0},{2,3},{3,2},{4,5},{5,4},{6,7},{7,6},{8,9},{9,8},{10,11... | collective-permute-start | bytes 3145736 | tf_op jit(solution)/shard_map/ppermute | solution.py:220
  63.4 13.4 %collective-permute-start.3 = (f32[56,64]{1,0:T(8,128)S(1)}, f32[56,64]{1,0:T(8,128)S(1)}, u32[]{:S(2)}, u32[]{:S(2)}) collective-permute-start(f32[56,64]{1,0:T(8,128)S(1)} %reshape.110.near_ref), channel_id=1, source_target_pairs={{0,2},{2,0},{1,3},{3,1},{4,6},{6,4},{5,7},{7,5},{8,10},{10,8},{9,1... | collective-permute-start | bytes 43016 | tf_op jit(solution)/shard_map/ppermute | solution.py:388
  71.2 22.4 %collective-permute-start.10 = (bf16[96,32,128]{2,1,0:T(8,128)(2,1)S(1)}, bf16[96,32,128]{2,1,0:T(8,128)(2,1)S(1)}, u32[]{:S(2)}, u32[]{:S(2)}) collective-permute-start(bf16[96,32,128]{2,1,0:T(8,128)(2,1)S(1)} %get-tuple-element.31.refs_0_), channel_id=1, source_target_pairs={{0,384},{1,13},{4,388},{5,1},{8,392},{9,5},{12,396},{13,9},{128,0}... | collective-permute-start | bytes 2359304 | tf_op jit(solution)/shard_map/ppermute | solution.py:216
  76.7 16.9 %collective-permute-start.13 = (bf16[96,32,128]{2,1,0:T(8,128)(2,1)S(1)}, bf16[96,32,128]{2,1,0:T(8,128)(2,1)S(1)}, u32[]{:S(2)}, u32[]{:S(2)}) collective-permute-start(bf16[96,32,128]{2,1,0:T(8,128)(2,1)S(1)} %get-tuple-element.32.refs_3_), channel_id=1, source_target_pairs={{0,128},{1,5},{4,132},{5,9},{8,136},{9,13},{12,140},{13,1},{128,25... | collective-permute-start | bytes 2359304 | tf_op jit(solution)/shard_map/ppermute | solution.py:216
  80.8 18.6 %collective-permute-start.14 = (bf16[96,32,128]{2,1,0:T(8,128)(2,1)S(1)}, bf16[96,32,128]{2,1,0:T(8,128)(2,1)S(1)}, u32[]{:S(2)}, u32[]{:S(2)}) collective-permute-start(bf16[96,32,128]{2,1,0:T(8,128)(2,1)S(1)} %collective-permute-done.11.refs_2_), channel_id=1, source_target_pairs={{0,128},{1,5},{4,132},{5,9},{8,136},{9,13},{12,140},{13,1},{128,25... | collective-permute-start | bytes 2359304 | tf_op jit(solution)/shard_map/ppermute | solution.py:216
  83.0 16.4 %collective-permute-start.15 = (bf16[96,32,128]{2,1,0:T(8,128)(2,1)S(1)}, bf16[96,32,128]{2,1,0:T(8,128)(2,1)S(1)}, u32[]{:S(2)}, u32[]{:S(2)}) collective-permute-start(bf16[96,32,128]{2,1,0:T(8,128)(2,1)S(1)} %collective-permute-done.12.refs_4_), channel_id=1, source_target_pairs={{0,384},{1,13},{4,388},{5,1},{8,392},{9,5},{12,396},{13,9},{128,0}... | collective-permute-start | bytes 2359304 | tf_op jit(solution)/shard_map/ppermute | solution.py:216
  105.6 6.6 %collective-permute-start.16 = (bf16[64,64,128]{2,1,0:T(8,128)(2,1)S(1)}, bf16[64,64,128]{2,1,0:T(8,128)(2,1)S(1)}, u32[]{:S(2)}, u32[]{:S(2)}) collective-permute-start(bf16[64,64,128]{2,1,0:T(8,128)(2,1)S(1)} %get-tuple-element.35), channel_id=1, source_target_pairs={{0,1},{1,0},{2,3},{3,2},{4,5},{5,4},{6,7},{7,6},{8,9},{9,8},{10,11... | collective-permute-start | bytes 3145736 | tf_op jit(solution)/shard_map/ppermute | solution.py:220
where the time goes:
time: 115 us; the launch traced here: 114 us
  starting transfers between devices  75.1 us (65%)
  Pallas kernels  18.4 us (16%)
  waiting for transfers between devices  15.7 us (14%)
  local copies, waits for them, and re-layouts  3.91 us (3%)
    ppermute x9, starting transfers between devices, along_side(): return lax.ppermute(v, ('y', 'x', 'core'), pairs)  32 us
    ppermute x4, starting transfers between devices, along_z(): return lax.ppermute(v, ('zl', 'zh', 'core'), pairs)  22.9 us
    ppermute x3, starting transfers between devices, swap_cores(): return lax.ppermute(v, 'core', [(0, 1), (1, 0)])  12.3 us
    ppermute x9, waiting for transfers between devices, along_side(): return lax.ppermute(v, ('y', 'x', 'core'), pairs)  11.5 us
    ppermute x1, starting transfers between devices, on_device(): distant = lax.ppermute(near, 'zh', [(0, 1), (1, 0)])  7.85 us
    pallas_call x1, Pallas kernels, sparse_call(): pl.pallas_call(body, out_shape=(pltpu.VMEM(filled.shape, filled.dtype), p...  6.21 us
    pallas_call x1, Pallas kernels, invert_call(): pl.pallas_call(body, out_shape=[jax.ShapeDtypeStruct((spots,), jnp.int32)...  6.18 us
    ppermute x4, waiting for transfers between devices, along_z(): return lax.ppermute(v, ('zl', 'zh', 'core'), pairs)  3.01 us
  transfers between devices with their start and end apart: 17, of which 5 were waited for; matrix products, arithmetic and copies ran while one was open for 3% of the time, Pallas kernels for 9%

commit v1 on v0

--- a/solution.py
+++ b/solution.py
@@ -243,17 +243,19 @@
     return lax.dynamic_index_in_dim(paired, core, paired.ndim - 4, keepdims=False)
 
 
-def gather_tiles(own, core, early):
+def gather_tiles(own, core, prepare, raw):
     _, slots = own.shape[:2]
     mine = of_core(own, core)
     far = along_z(own, 3)
     middle = along_z(own, 2)
     near = along_z(own, 1)
     opposite = along_z(of_core(middle, core), 2)
-    near, middle, far, early = lax.optimization_barrier((near, middle, far, early))
+    near, middle, far, raw = lax.optimization_barrier((near, middle, far, raw))
     side = jnp.stack([near, middle, far])
+    early = prepare(*raw)
     theirs = swap_cores(of_core(side, 1 - core))
     line = jnp.concatenate([mine[None], of_core(side, core), opposite[None], theirs], axis=0)
+    line, early = lax.optimization_barrier((line, early))
     line = line.transpose(1, 0, 2, 3, 4).reshape(2, NZ * slots, HALF, 2 * BLOCK)
     across, back, ahead = along_side(line, 2, 0), along_side(line, 1, 0), along_side(line, -1, 0)
     planes = join(line, ahead, across, back)
@@ -375,13 +377,14 @@
         paired = table.reshape(2, 2, columns * per_column)
         return lax.dynamic_index_in_dim(paired, core, 1, keepdims=False).reshape(-1)
 
-    rows = of_runs(block_rows)
-    places = tile_places(block_slot, slots, y, zl, x, core).reshape(runs, columns * per_column)
-    second = jnp.arange(runs)[:, None] // 2 * (NX * NY * NZ * slots)
-    places = of_runs(places + second)
-    near = penalty.reshape(columns, BLOCK)
+    def prepare(block_rows, block_slot, penalty):
+        places = tile_places(block_slot, slots, y, zl, x, core).reshape(runs, columns * per_column)
+        second = jnp.arange(runs)[:, None] // 2 * (NX * NY * NZ * slots)
+        return of_runs(block_rows), of_runs(places + second), penalty.reshape(columns, BLOCK), zh.reshape(1)
+
     own = pack_tiles(weight_tiles)
-    tiles, (rows, places, near, high) = gather_tiles(own, core, (rows, places, near, zh.reshape(1)))
+    raw = block_rows, block_slot, penalty
+    tiles, (rows, places, near, high) = gather_tiles(own, core, prepare, raw)
     gain = norm_gain.reshape(1, width)
     features, inverse = norm_call(tokens, gain)
     other = swap_cores(features)

time: 115 us -> 112 us (0.974)
  waiting for transfers between devices: 15.7 us -> 12.8 us
    ppermute x4, waiting for transfers between devices: 3.01 us -> 0.11 us  [along_z(): return lax.ppermute(v, ('zl', 'zh', 'core'), pairs)]
    ppermute x3, starting transfers between devices: 12.3 us -> 9.87 us  [swap_cores(): return lax.ppermute(v, 'core', [(0, 1), (1, 0)])]
    ppermute x4, starting transfers between devices: 22.9 us -> 24.8 us  [along_z(): return lax.ppermute(v, ('zl', 'zh', 'core'), pairs)]
where the time goes in v1:
time: 112 us; the launch traced here: 111 us
  starting transfers between devices  74.4 us (66%)
  Pallas kernels  18.4 us (16%)
  waiting for transfers between devices  12.8 us (11%)
  local copies, waits for them, and re-layouts  3.9 us (3%)
    ppermute x9, starting transfers between devices, along_side(): return lax.ppermute(v, ('y', 'x', 'core'), pairs)  32 us
    ppermute x4, starting transfers between devices, along_z(): return lax.ppermute(v, ('zl', 'zh', 'core'), pairs)  24.8 us
    ppermute x9, waiting for transfers between devices, along_side(): return lax.ppermute(v, ('y', 'x', 'core'), pairs)  11.5 us
    ppermute x3, starting transfers between devices, swap_cores(): return lax.ppermute(v, 'core', [(0, 1), (1, 0)])  9.87 us
    ppermute x1, starting transfers between devices, on_device(): distant = lax.ppermute(near, 'zh', [(0, 1), (1, 0)])  7.75 us
    pallas_call x1, Pallas kernels, sparse_call(): pl.pallas_call(body, out_shape=(pltpu.VMEM(filled.shape, filled.dtype), p...  6.21 us
    pallas_call x1, Pallas kernels, invert_call(): pl.pallas_call(body, out_shape=[jax.ShapeDtypeStruct((spots,), jnp.int32)...  6.18 us
    pallas_call x1, Pallas kernels, sparse_call(): pl.pallas_call(keep_kernel, out_shape=pltpu.VMEM((row_blocks, BLOCK, coun...  2.65 us
  transfers between devices with their start and end apart: 17, of which 5 were waited for; matrix products, arithmetic and copies ran while one was open for 3% of the time, Pallas kernels for 9%

profile of v1, /device:TPU:1, one launch (start us, length us, event | category | flops | bytes accessed | tf_op | source)
XLA Modules:
  0.0 110.9 jit_solution(17572774174221838788)
XLA Ops:
  0.0 0.0 copy-start
  0.0 0.0 copy-start.1
  0.0 1.2 %reshape.104 = bf16[4,3,2,32,64]{4,3,2,0,1:T(8,128)(2,1)S(1)} reshape(bf16[4,3,4096]{2,0,1:T(4,128)(2,1)} %param.9) | data formatting | bytes 196608 | tf_op jit(solution)/shard_map/reshape | solution.py:366
  1.2 0.2 copy.16
  1.4 0.1 reshape.105
  1.5 12.8 %collective-permute-start.2 = (bf16[4,3,32,128]{3,2,1,0:T(8,128)(2,1)S(1)}, bf16[4,3,32,128]{3,2,1,0:T(8,128)(2,1)S(1)}, u32[]{:S(2)}, u32[]{:S(2)}) collective-permute-start(bf16[4,3,32,128]{3,2,1,0:T(8,128)(2,1)S(1)} %reshape.105), channel_id=1, source_target_pairs={{0,48},{1,83},{16,64},{17,99},{32,80},{33,115},{48,96},{49,1},{64,... | collective-permute-start | bytes 294920 | tf_op jit(solution)/shard_map/ppermute | solution.py:206
  14.4 4.3 %collective-permute-start.1 = (bf16[4,3,32,128]{3,2,1,0:T(8,128)(2,1)S(1)}, bf16[4,3,32,128]{3,2,1,0:T(8,128)(2,1)S(1)}, u32[]{:S(2)}, u32[]{:S(2)}) collective-permute-start(bf16[4,3,32,128]{3,2,1,0:T(8,128)(2,1)S(1)} %reshape.105), channel_id=1, source_target_pairs={{0,32},{1,99},{16,48},{17,115},{32,64},{33,1},{48,80},{49,17},{64,... | collective-permute-start | bytes 294920 | tf_op jit(solution)/shard_map/ppermute | solution.py:206
  18.7 2.6 %collective-permute-start = (bf16[4,3,32,128]{3,2,1,0:T(8,128)(2,1)S(1)}, bf16[4,3,32,128]{3,2,1,0:T(8,128)(2,1)S(1)}, u32[]{:S(2)}, u32[]{:S(2)}) collective-permute-start(bf16[4,3,32,128]{3,2,1,0:T(8,128)(2,1)S(1)} %reshape.105), channel_id=1, source_target_pairs={{0,16},{1,115},{16,32},{17,1},{32,48},{33,17},{48,64},{49,33},{64,... | collective-permute-start | bytes 294920 | tf_op jit(solution)/shard_map/ppermute | solution.py:206
  21.3 0.1 reshape_reshape.3
  21.5 0.1 constant_dynamic-slice_fusion
  21.6 0.1 collective-permute-done.1
  21.7 5.0 %collective-permute-start.3 = (bf16[2,3,32,128]{3,2,1,0:T(8,128)(2,1)S(1)}, bf16[2,3,32,128]{3,2,1,0:T(8,128)(2,1)S(1)}, u32[]{:S(2)}, u32[]{:S(2)}) collective-permute-start(bf16[2,3,32,128]{3,2,1,0:T(8,128)(2,1)S(1)} %dynamic-slice_bitcast_fusion.2), channel_id=1, source_target_pairs={{0,32},{1,99},{16,48},{17,115},{32,64},{33,1},{48,80},{49,17},{64,... | collective-permute-start | bytes 147464 | tf_op jit(solution)/shard_map/ppermute | solution.py:206
  26.7 0.0 collective-permute-done.2
  26.7 0.0 collective-permute-done
  26.8 1.9 %collective-permute-start.4 = (bf16[3,2,3,32,128]{4,3,2,1,0:T(8,128)(2,1)S(1)}, bf16[3,2,3,32,128]{4,3,2,1,0:T(8,128)(2,1)S(1)}, u32[]{:S(2)}, u32[]{:S(2)}) collective-permute-start(bf16[3,2,3,32,128]{4,3,2,1,0:T(8,128)(2,1)S(1)} %get-tuple-element.46), channel_id=1, source_target_pairs={{0,1},{1,0},{2,3},{3,2},{4,5},{5,4},{6,7},{7,6},{8,9},{9,8},{10,11... | collective-permute-start | bytes 442376 | tf_op jit(solution)/shard_map/ppermute | solution.py:220
  28.7 0.7 fusion.9
  29.4 0.1 copy.13
  29.6 0.1 reshape.109
  29.7 0.8 copy.12
  30.5 0.1 reshape.107
  30.6 0.1 fusion.14
  30.7 0.8 reshape.111.near_ref
  31.5 0.1 reshape.110.refs_0_
  31.6 0.1 reshape.108.refs_1_
  31.7 0.0 collective-permute-done.3
  31.7 0.0 collective-permute-done.4
  31.7 0.1 pad_maximum_fusion
  31.8 3.2 %collective-permute-start.9 = (bf16[2,24,32,128]{3,2,1,0:T(8,128)(2,1)S(1)}, bf16[2,24,32,128]{3,2,1,0:T(8,128)(2,1)S(1)}, u32[]{:S(2)}, u32[]{:S(2)}) collective-permute-start(bf16[2,24,32,128]{3,2,1,0:T(8,128)(2,1)S(1)} %bitcast.27), channel_id=1, source_target_pairs={{0,4},{1,129},{4,8},{5,133},{8,12},{9,137},{12,0},{13,141},{128,13... | collective-permute-start | bytes 1179656 | tf_op jit(solution)/shard_map/ppermute | solution.py:216
  35.0 4.5 %collective-permute-start.8 = (bf16[2,24,32,128]{3,2,1,0:T(8,128)(2,1)S(1)}, bf16[2,24,32,128]{3,2,1,0:T(8,128)(2,1)S(1)}, u32[]{:S(2)}, u32[]{:S(2)}) collective-permute-start(bf16[2,24,32,128]{3,2,1,0:T(8,128)(2,1)S(1)} %bitcast.28), channel_id=1, source_target_pairs={{0,8},{1,257},{4,12},{5,261},{8,0},{9,265},{12,4},{13,269},{128,13... | collective-permute-start | bytes 1179656 | tf_op jit(solution)/shard_map/ppermute | solution.py:216
  39.5 3.0 %collective-permute-start.7 = (bf16[2,24,32,128]{3,2,1,0:T(8,128)(2,1)S(1)}, bf16[2,24,32,128]{3,2,1,0:T(8,128)(2,1)S(1)}, u32[]{:S(2)}, u32[]{:S(2)}) collective-permute-start(bf16[2,24,32,128]{3,2,1,0:T(8,128)(2,1)S(1)} %bitcast.29), channel_id=1, source_target_pairs={{0,12},{1,385},{4,0},{5,389},{8,4},{9,393},{12,8},{13,397},{128,14... | collective-permute-start | bytes 1179656 | tf_op jit(solution)/shard_map/ppermute | solution.py:216
  42.5 0.0 collective-permute-done.9.back_ref
  42.5 4.7 %collective-permute-done.8.across_ref = bf16[2,24,32,128]{3,2,1,0:T(8,128)(2,1)S(1)} collective-permute-done((bf16[2,24,32,128]{3,2,1,0:T(8,128)(2,1)S(1)}, bf16[2,24,32,128]{3,2,1,0:T(8,128)(2,1)S(1)}, u32[]{:S(2)}, u32[]{:S(2)}) %collective-permute-start.8) | collective-permute-done | bytes 393248 | tf_op jit(solution)/shard_map/ppermute | solution.py:216
  47.3 1.3 %collective-permute-done.7.ahead_ref = bf16[2,24,32,128]{3,2,1,0:T(8,128)(2,1)S(1)} collective-permute-done((bf16[2,24,32,128]{3,2,1,0:T(8,128)(2,1)S(1)}, bf16[2,24,32,128]{3,2,1,0:T(8,128)(2,1)S(1)}, u32[]{:S(2)}, u32[]{:S(2)}) %collective-permute-start.7) | collective-permute-done | bytes 393248 | tf_op jit(solution)/shard_map/ppermute | solution.py:216
  48.6 0.1 shard_map.67
  48.7 3.1 %collective-permute-start.11 = (bf16[96,32,128]{2,1,0:T(8,128)(2,1)S(1)}, bf16[96,32,128]{2,1,0:T(8,128)(2,1)S(1)}, u32[]{:S(2)}, u32[]{:S(2)}) collective-permute-start(bf16[96,32,128]{2,1,0:T(8,128)(2,1)S(1)} %get-tuple-element.39.refs_0_), channel_id=1, source_target_pairs={{0,128},{1,5},{4,132},{5,9},{8,136},{9,13},{12,140},{13,1},{128,25... | collective-permute-start | bytes 2359304 | tf_op jit(solution)/shard_map/ppermute | solution.py:216
  51.8 3.4 %collective-permute-start.12 = (bf16[96,32,128]{2,1,0:T(8,128)(2,1)S(1)}, bf16[96,32,128]{2,1,0:T(8,128)(2,1)S(1)}, u32[]{:S(2)}, u32[]{:S(2)}) collective-permute-start(bf16[96,32,128]{2,1,0:T(8,128)(2,1)S(1)} %get-tuple-element.40.refs_3_), channel_id=1, source_target_pairs={{0,384},{1,13},{4,388},{5,1},{8,392},{9,5},{12,396},{13,9},{128,0}... | collective-permute-start | bytes 2359304 | tf_op jit(solution)/shard_map/ppermute | solution.py:216
  55.2 0.0 copy-done
  55.2 0.0 copy-done.1
  55.2 0.6 shard_map.66
  55.9 4.0 %collective-permute-start.6 = (bf16[4096,128]{1,0:T(8,128)(2,1)S(1)}, bf16[4096,128]{1,0:T(8,128)(2,1)S(1)}, u32[]{:S(2)}, u32[]{:S(2)}) collective-permute-start(bf16[4096,128]{1,0:T(8,128)(2,1)S(1)} %get-tuple-element.37), channel_id=1, source_target_pairs={{0,1},{1,0},{2,3},{3,2},{4,5},{5,4},{6,7},{7,6},{8,9},{9,8},{10,11... | collective-permute-start | bytes 3145736 | tf_op jit(solution)/shard_map/ppermute | solution.py:220
  59.9 7.8 %collective-permute-start.5 = (f32[56,64]{1,0:T(8,128)S(1)}, f32[56,64]{1,0:T(8,128)S(1)}, u32[]{:S(2)}, u32[]{:S(2)}) collective-permute-start(f32[56,64]{1,0:T(8,128)S(1)} %reshape.111.near_ref), channel_id=1, source_target_pairs={{0,2},{2,0},{1,3},{3,1},{4,6},{6,4},{5,7},{7,5},{8,10},{10,8},{9,1... | collective-permute-start | bytes 43016 | tf_op jit(solution)/shard_map/ppermute | solution.py:391
  67.6 4.3 %collective-permute-start.10 = (bf16[96,32,128]{2,1,0:T(8,128)(2,1)S(1)}, bf16[96,32,128]{2,1,0:T(8,128)(2,1)S(1)}, u32[]{:S(2)}, u32[]{:S(2)}) collective-permute-start(bf16[96,32,128]{2,1,0:T(8,128)(2,1)S(1)} %get-tuple-element.39.refs_0_), channel_id=1, source_target_pairs={{0,384},{1,13},{4,388},{5,1},{8,392},{9,5},{12,396},{13,9},{128,0}... | collective-permute-start | bytes 2359304 | tf_op jit(solution)/shard_map/ppermute | solution.py:216
  72.0 1.3 %collective-permute-done.5.far_ref = f32[56,64]{1,0:T(8,128)S(1)} collective-permute-done((f32[56,64]{1,0:T(8,128)S(1)}, f32[56,64]{1,0:T(8,128)S(1)}, u32[]{:S(2)}, u32[]{:S(2)}) %collective-permute-start.5) | collective-permute-done | bytes 14368 | tf_op jit(solution)/shard_map/ppermute | solution.py:391
  73.2 4.0 %collective-permute-start.13 = (bf16[96,32,128]{2,1,0:T(8,128)(2,1)S(1)}, bf16[96,32,128]{2,1,0:T(8,128)(2,1)S(1)}, u32[]{:S(2)}, u32[]{:S(2)}) collective-permute-start(bf16[96,32,128]{2,1,0:T(8,128)(2,1)S(1)} %get-tuple-element.40.refs_3_), channel_id=1, source_target_pairs={{0,128},{1,5},{4,132},{5,9},{8,136},{9,13},{12,140},{13,1},{128,25... | collective-permute-start | bytes 2359304 | tf_op jit(solution)/shard_map/ppermute | solution.py:216
  77.3 0.0 collective-permute-done.11.refs_2_
  77.3 2.2 %collective-permute-start.14 = (bf16[96,32,128]{2,1,0:T(8,128)(2,1)S(1)}, bf16[96,32,128]{2,1,0:T(8,128)(2,1)S(1)}, u32[]{:S(2)}, u32[]{:S(2)}) collective-permute-start(bf16[96,32,128]{2,1,0:T(8,128)(2,1)S(1)} %collective-permute-done.11.refs_2_), channel_id=1, source_target_pairs={{0,128},{1,5},{4,132},{5,9},{8,136},{9,13},{12,140},{13,1},{128,25... | collective-permute-start | bytes 2359304 | tf_op jit(solution)/shard_map/ppermute | solution.py:216
  79.5 0.0 collective-permute-done.12.refs_4_
  79.5 4.3 %collective-permute-start.15 = (bf16[96,32,128]{2,1,0:T(8,128)(2,1)S(1)}, bf16[96,32,128]{2,1,0:T(8,128)(2,1)S(1)}, u32[]{:S(2)}, u32[]{:S(2)}) collective-permute-start(bf16[96,32,128]{2,1,0:T(8,128)(2,1)S(1)} %collective-permute-done.12.refs_4_), channel_id=1, source_target_pairs={{0,384},{1,13},{4,388},{5,1},{8,392},{9,5},{12,396},{13,9},{128,0}... | collective-permute-start | bytes 2359304 | tf_op jit(solution)/shard_map/ppermute | solution.py:216
  83.8 6.2 %shard_map.64 = (s32[512]{0:T(512)S(1)}, s32[512]{0:T(512)S(1)}) custom-call(s32[448]{0:T(512)S(1)} %reshape.110.refs_0_, s32[448]{0:T(512)S(1)} %reshape.108.refs_1_), custom_call_target="tpu_custom_call" | custom-call | tf_op jit(solution)/shard_map/pallas_call | solution.py:68
  90.0 0.2 shard_map.65.refs_4_
  90.1 0.0 collective-permute-done.10.refs_1_
  90.2 0.0 collective-permute-done.13.refs_5_
  90.2 0.3 shard_map.68.refs_7_
  90.5 0.0 collective-permute-done.6
  90.5 5.4 %collective-permute-done.14.refs_8_ = bf16[96,32,128]{2,1,0:T(8,128)(2,1)S(1)} collective-permute-done((bf16[96,32,128]{2,1,0:T(8,128)(2,1)S(1)}, bf16[96,32,128]{2,1,0:T(8,128)(2,1)S(1)}, u32[]{:S(2)}, u32[]{:S(2)}) %collective-permute-start.14) | collective-permute-done | bytes 786464 | tf_op jit(solution)/shard_map/ppermute | solution.py:216
  95.9 0.0 collective-permute-done.15.refs_9_
  95.9 6.2 %shard_map.69 = (bf16[769,32,128]{2,1,0:T(8,128)(2,1)S(1)}, bf16[112,64,256]{2,1,0:T(8,128)(2,1)S(1)}, bf16[64,64,128]{2,1,0:T(8,128)(2,1)S(1)}) custom-call(s32[448]{0:T(512)S(1)} %reshape.110.refs_0_, s32[448]{0:T(512)S(1)} %reshape.108.refs_1_, s32[512]{0:T(512)S(1)} %get-tuple-element.33.refs_2_.tile_ref, ...), custom_call_target="tpu_custom_call", output_to_operand_aliasing={{0}: (7, {})} | custom-call | tf_op jit(solution)/shard_map/pallas_call | solution.py:289
  102.1 3.9 %collective-permute-start.16 = (bf16[64,64,128]{2,1,0:T(8,128)(2,1)S(1)}, bf16[64,64,128]{2,1,0:T(8,128)(2,1)S(1)}, u32[]{:S(2)}, u32[]{:S(2)}) collective-permute-start(bf16[64,64,128]{2,1,0:T(8,128)(2,1)S(1)} %get-tuple-element.43), channel_id=1, source_target_pairs={{0,1},{1,0},{2,3},{3,2},{4,5},{5,4},{6,7},{7,6},{8,9},{9,8},{10,11... | collective-permute-start | bytes 3145736 | tf_op jit(solution)/shard_map/ppermute | solution.py:220
  106.0 2.6 %shard_map.70 = f32[64,64,128]{2,1,0:T(8,128)S(1)} custom-call(s32[512]{0:T(512)S(1)} %get-tuple-element.33.refs_2_.tile_ref, s32[512]{0:T(512)S(1)} %get-tuple-element.34.refs_3_.column_ref, bf16[769,32,128]{2,1,0:T(8,128)(2,1)S(1)} %get-tuple-element.41.w_ref, bf16[112,64,256]{2,1,0:T(8,128)(2,1)S(1)} %get-tuple-element.42.grad_ref), custom_call_target="tpu_custom_call" | custom-call | tf_op jit(solution)/shard_map/pallas_call | solution.py:305
  108.7 0.0 collective-permute-done.16
  108.7 2.2 %shard_map.71 = bf16[128,4096]{1,0:T(8,128)(2,1)} custom-call(f32[4096,128]{1,0:T(8,128)S(1)} %bitcast.26, bf16[4096,128]{1,0:T(8,128)(2,1)S(1)} %bitcast.33, bf16[128,4096]{1,0:T(8,128)(2,1)S(1)} %copy-done, f32[1,4096]{1,0:T(1,128)S(1)} %bitcast.35, f32[128,1]{1,0:T(8,128)S(1)} %get-tuple-element.44.inverse_ref), custom_call_target="tpu_custom_call" | custom-call | tf_op jit(solution)/shard_map/pallas_call | solution.py:331
  (6 shorter events, 0.1 us)
Async XLA Ops:
  0.0 55.2 %copy-start = (bf16[128,4096]{1,0:T(8,128)(2,1)S(1)}, bf16[128,4096]{1,0:T(8,128)(2,1)}, u32[]{:S(2)}) copy-start(bf16[128,4096]{1,0:T(8,128)(2,1)} %tokens_ref.3) | copy-start | bytes 3145732
  0.0 55.2 %copy-start.1 = (f32[4096]{0:T(1024)S(1)}, f32[4096]{0:T(1024)}, u32[]{:S(2)}) copy-start(f32[4096]{0:T(1024)} %param.7) | copy-start | bytes 49156
  1.5 25.2 %collective-permute-start.2 = (bf16[4,3,32,128]{3,2,1,0:T(8,128)(2,1)S(1)}, bf16[4,3,32,128]{3,2,1,0:T(8,128)(2,1)S(1)}, u32[]{:S(2)}, u32[]{:S(2)}) collective-permute-start(bf16[4,3,32,128]{3,2,1,0:T(8,128)(2,1)S(1)} %reshape.105), channel_id=1, source_target_pairs={{0,48},{1,83},{16,64},{17,99},{32,80},{33,115},{48,96},{49,1},{64,... | collective-permute-start | bytes 294920 | tf_op jit(solution)/shard_map/ppermute | solution.py:206
  14.4 7.3 %collective-permute-start.1 = (bf16[4,3,32,128]{3,2,1,0:T(8,128)(2,1)S(1)}, bf16[4,3,32,128]{3,2,1,0:T(8,128)(2,1)S(1)}, u32[]{:S(2)}, u32[]{:S(2)}) collective-permute-start(bf16[4,3,32,128]{3,2,1,0:T(8,128)(2,1)S(1)} %reshape.105), channel_id=1, source_target_pairs={{0,32},{1,99},{16,48},{17,115},{32,64},{33,1},{48,80},{49,17},{64,... | collective-permute-start | bytes 294920 | tf_op jit(solution)/shard_map/ppermute | solution.py:206
  18.7 8.0 %collective-permute-start = (bf16[4,3,32,128]{3,2,1,0:T(8,128)(2,1)S(1)}, bf16[4,3,32,128]{3,2,1,0:T(8,128)(2,1)S(1)}, u32[]{:S(2)}, u32[]{:S(2)}) collective-permute-start(bf16[4,3,32,128]{3,2,1,0:T(8,128)(2,1)S(1)} %reshape.105), channel_id=1, source_target_pairs={{0,16},{1,115},{16,32},{17,1},{32,48},{33,17},{48,64},{49,33},{64,... | collective-permute-start | bytes 294920 | tf_op jit(solution)/shard_map/ppermute | solution.py:206
  21.7 10.0 %collective-permute-start.3 = (bf16[2,3,32,128]{3,2,1,0:T(8,128)(2,1)S(1)}, bf16[2,3,32,128]{3,2,1,0:T(8,128)(2,1)S(1)}, u32[]{:S(2)}, u32[]{:S(2)}) collective-permute-start(bf16[2,3,32,128]{3,2,1,0:T(8,128)(2,1)S(1)} %dynamic-slice_bitcast_fusion.2), channel_id=1, source_target_pairs={{0,32},{1,99},{16,48},{17,115},{32,64},{33,1},{48,80},{49,17},{64,... | collective-permute-start | bytes 147464 | tf_op jit(solution)/shard_map/ppermute | solution.py:206
  26.8 4.9 %collective-permute-start.4 = (bf16[3,2,3,32,128]{4,3,2,1,0:T(8,128)(2,1)S(1)}, bf16[3,2,3,32,128]{4,3,2,1,0:T(8,128)(2,1)S(1)}, u32[]{:S(2)}, u32[]{:S(2)}) collective-permute-start(bf16[3,2,3,32,128]{4,3,2,1,0:T(8,128)(2,1)S(1)} %get-tuple-element.46), channel_id=1, source_target_pairs={{0,1},{1,0},{2,3},{3,2},{4,5},{5,4},{6,7},{7,6},{8,9},{9,8},{10,11... | collective-permute-start | bytes 442376 | tf_op jit(solution)/shard_map/ppermute | solution.py:220
  31.8 10.7 %collective-permute-start.9 = (bf16[2,24,32,128]{3,2,1,0:T(8,128)(2,1)S(1)}, bf16[2,24,32,128]{3,2,1,0:T(8,128)(2,1)S(1)}, u32[]{:S(2)}, u32[]{:S(2)}) collective-permute-start(bf16[2,24,32,128]{3,2,1,0:T(8,128)(2,1)S(1)} %bitcast.27), channel_id=1, source_target_pairs={{0,4},{1,129},{4,8},{5,133},{8,12},{9,137},{12,0},{13,141},{128,13... | collective-permute-start | bytes 1179656 | tf_op jit(solution)/shard_map/ppermute | solution.py:216
  35.0 12.3 %collective-permute-start.8 = (bf16[2,24,32,128]{3,2,1,0:T(8,128)(2,1)S(1)}, bf16[2,24,32,128]{3,2,1,0:T(8,128)(2,1)S(1)}, u32[]{:S(2)}, u32[]{:S(2)}) collective-permute-start(bf16[2,24,32,128]{3,2,1,0:T(8,128)(2,1)S(1)} %bitcast.28), channel_id=1, source_target_pairs={{0,8},{1,257},{4,12},{5,261},{8,0},{9,265},{12,4},{13,269},{128,13... | collective-permute-start | bytes 1179656 | tf_op jit(solution)/shard_map/ppermute | solution.py:216
  39.5 9.1 %collective-permute-start.7 = (bf16[2,24,32,128]{3,2,1,0:T(8,128)(2,1)S(1)}, bf16[2,24,32,128]{3,2,1,0:T(8,128)(2,1)S(1)}, u32[]{:S(2)}, u32[]{:S(2)}) collective-permute-start(bf16[2,24,32,128]{3,2,1,0:T(8,128)(2,1)S(1)} %bitcast.29), channel_id=1, source_target_pairs={{0,12},{1,385},{4,0},{5,389},{8,4},{9,393},{12,8},{13,397},{128,14... | collective-permute-start | bytes 1179656 | tf_op jit(solution)/shard_map/ppermute | solution.py:216
  48.7 28.6 %collective-permute-start.11 = (bf16[96,32,128]{2,1,0:T(8,128)(2,1)S(1)}, bf16[96,32,128]{2,1,0:T(8,128)(2,1)S(1)}, u32[]{:S(2)}, u32[]{:S(2)}) collective-permute-start(bf16[96,32,128]{2,1,0:T(8,128)(2,1)S(1)} %get-tuple-element.39.refs_0_), channel_id=1, source_target_pairs={{0,128},{1,5},{4,132},{5,9},{8,136},{9,13},{12,140},{13,1},{128,25... | collective-permute-start | bytes 2359304 | tf_op jit(solution)/shard_map/ppermute | solution.py:216
  51.8 27.7 %collective-permute-start.12 = (bf16[96,32,128]{2,1,0:T(8,128)(2,1)S(1)}, bf16[96,32,128]{2,1,0:T(8,128)(2,1)S(1)}, u32[]{:S(2)}, u32[]{:S(2)}) collective-permute-start(bf16[96,32,128]{2,1,0:T(8,128)(2,1)S(1)} %get-tuple-element.40.refs_3_), channel_id=1, source_target_pairs={{0,384},{1,13},{4,388},{5,1},{8,392},{9,5},{12,396},{13,9},{128,0}... | collective-permute-start | bytes 2359304 | tf_op jit(solution)/shard_map/ppermute | solution.py:216
  55.9 34.6 %collective-permute-start.6 = (bf16[4096,128]{1,0:T(8,128)(2,1)S(1)}, bf16[4096,128]{1,0:T(8,128)(2,1)S(1)}, u32[]{:S(2)}, u32[]{:S(2)}) collective-permute-start(bf16[4096,128]{1,0:T(8,128)(2,1)S(1)} %get-tuple-element.37), channel_id=1, source_target_pairs={{0,1},{1,0},{2,3},{3,2},{4,5},{5,4},{6,7},{7,6},{8,9},{9,8},{10,11... | collective-permute-start | bytes 3145736 | tf_op jit(solution)/shard_map/ppermute | solution.py:220
  59.9 13.3 %collective-permute-start.5 = (f32[56,64]{1,0:T(8,128)S(1)}, f32[56,64]{1,0:T(8,128)S(1)}, u32[]{:S(2)}, u32[]{:S(2)}) collective-permute-start(f32[56,64]{1,0:T(8,128)S(1)} %reshape.111.near_ref), channel_id=1, source_target_pairs={{0,2},{2,0},{1,3},{3,1},{4,6},{6,4},{5,7},{7,5},{8,10},{10,8},{9,1... | collective-permute-start | bytes 43016 | tf_op jit(solution)/shard_map/ppermute | solution.py:391
  67.6 22.5 %collective-permute-start.10 = (bf16[96,32,128]{2,1,0:T(8,128)(2,1)S(1)}, bf16[96,32,128]{2,1,0:T(8,128)(2,1)S(1)}, u32[]{:S(2)}, u32[]{:S(2)}) collective-permute-start(bf16[96,32,128]{2,1,0:T(8,128)(2,1)S(1)} %get-tuple-element.39.refs_0_), channel_id=1, source_target_pairs={{0,384},{1,13},{4,388},{5,1},{8,392},{9,5},{12,396},{13,9},{128,0}... | collective-permute-start | bytes 2359304 | tf_op jit(solution)/shard_map/ppermute | solution.py:216
  73.2 16.9 %collective-permute-start.13 = (bf16[96,32,128]{2,1,0:T(8,128)(2,1)S(1)}, bf16[96,32,128]{2,1,0:T(8,128)(2,1)S(1)}, u32[]{:S(2)}, u32[]{:S(2)}) collective-permute-start(bf16[96,32,128]{2,1,0:T(8,128)(2,1)S(1)} %get-tuple-element.40.refs_3_), channel_id=1, source_target_pairs={{0,128},{1,5},{4,132},{5,9},{8,136},{9,13},{12,140},{13,1},{128,25... | collective-permute-start | bytes 2359304 | tf_op jit(solution)/shard_map/ppermute | solution.py:216
  77.3 18.6 %collective-permute-start.14 = (bf16[96,32,128]{2,1,0:T(8,128)(2,1)S(1)}, bf16[96,32,128]{2,1,0:T(8,128)(2,1)S(1)}, u32[]{:S(2)}, u32[]{:S(2)}) collective-permute-start(bf16[96,32,128]{2,1,0:T(8,128)(2,1)S(1)} %collective-permute-done.11.refs_2_), channel_id=1, source_target_pairs={{0,128},{1,5},{4,132},{5,9},{8,136},{9,13},{12,140},{13,1},{128,25... | collective-permute-start | bytes 2359304 | tf_op jit(solution)/shard_map/ppermute | solution.py:216
  79.5 16.4 %collective-permute-start.15 = (bf16[96,32,128]{2,1,0:T(8,128)(2,1)S(1)}, bf16[96,32,128]{2,1,0:T(8,128)(2,1)S(1)}, u32[]{:S(2)}, u32[]{:S(2)}) collective-permute-start(bf16[96,32,128]{2,1,0:T(8,128)(2,1)S(1)} %collective-permute-done.12.refs_4_), channel_id=1, source_target_pairs={{0,384},{1,13},{4,388},{5,1},{8,392},{9,5},{12,396},{13,9},{128,0}... | collective-permute-start | bytes 2359304 | tf_op jit(solution)/shard_map/ppermute | solution.py:216
  102.1 6.6 %collective-permute-start.16 = (bf16[64,64,128]{2,1,0:T(8,128)(2,1)S(1)}, bf16[64,64,128]{2,1,0:T(8,128)(2,1)S(1)}, u32[]{:S(2)}, u32[]{:S(2)}) collective-permute-start(bf16[64,64,128]{2,1,0:T(8,128)(2,1)S(1)} %get-tuple-element.43), channel_id=1, source_target_pairs={{0,1},{1,0},{2,3},{3,2},{4,5},{5,4},{6,7},{7,6},{8,9},{9,8},{10,11... | collective-permute-start | bytes 3145736 | tf_op jit(solution)/shard_map/ppermute | solution.py:220
